TPU v7x, 32 devices: a whole 2x2x4 slice. The times are simulated.
32 devices in a mesh: group: 2 (over y), context: 4 (over z), head: 4 (over x, core).
Axes of the slice: x: 2, y: 2, z: 4, core: 2. Of those that a mesh axis runs over, the one named last changes fastest.
Arguments:
- dn_query: bfloat16 [1024, 2048], P(('group', 'context'), 'head'), parts along dimension 0, may hold values from -6 to 6
- dn_key: bfloat16 [1024, 2048], P(('group', 'context'), 'head'), parts along dimension 0, may hold values from -6 to 6
- dn_value: bfloat16 [1024, 4096], P(('group', 'context'), 'head'), parts along dimension 0, may hold values from -6 to 6
- dn_gate: bfloat16 [1024, 4096], P(('group', 'context'), 'head'), parts along dimension 0, may hold values from -6 to 6
- dn_beta_logit: float32 [1024, 32], P(('group', 'context'), 'head'), parts along dimension 0, may hold values from -6 to 6
- dn_decay: float32 [1024, 32], P(('group', 'context'), 'head'), parts along dimension 0, may hold values from -1 to 0
- dn_norm_gain: float32 [128], replicated, may hold values from 0.1 to 1.9
- prefix_state: bfloat16 [4, 32, 128, 128], P('group', 'head', 'context'), parts along dimension 0, may hold values from -6 to 6
- at_query: bfloat16 [1024, 4096], P(('group', 'context'), 'head'), parts along dimension 0, may hold values from -6 to 6
- at_gate: bfloat16 [1024, 4096], P(('group', 'context'), 'head'), parts along dimension 0, may hold values from -6 to 6
- at_key: bfloat16 [1024, 512], P(('group', 'context')), parts along dimension 0, may hold values from -6 to 6
- at_value: bfloat16 [1024, 512], P(('group', 'context')), parts along dimension 0, may hold values from -6 to 6
- prefix_key: bfloat16 [16, 64, 512], P(('group', 'context')), parts along dimension 0, may hold values from -6 to 6
- prefix_value: bfloat16 [16, 64, 512], P(('group', 'context')), parts along dimension 0, may hold values from -6 to 6
- req_len: int32 [8], P('group'), parts along dimension 0, may hold values from 1 to 256, 512 in all
- req_prefix: int32 [8], P('group'), parts along dimension 0, may hold values from 0 to 1, as said below
- req_offset: int32 [8], P('group'), parts along dimension 0, may hold values from 64 to 256, as said below
- block_table: int32 [16], P('group'), parts along dimension 0, may hold values from 0 to 7, each once
Outputs:
- dn_out: bfloat16 [1024, 4096], P(('group', 'context'), 'head'), parts along dimension 0
- at_out: bfloat16 [1024, 4096], P(('group', 'context'), 'head'), parts along dimension 0
There are 2 independent parts, one for each index of `group`. A program takes and returns all parts, laid end to end along the dimension named above; an argument that names none is the same for every part. Nothing has to cross between parts.
Inputs may be any that keep to these rules, and one draw needn't show every extreme that they name: `req_len`: requests lie one after another in row order; the longest has exactly 256 new tokens. `req_prefix`: every prefix is extended by one or more requests. `req_offset`: equal for the requests of one prefix: the number of its cached positions; one prefix holds 256, another from a quarter to a half of 256. `block_table`: entry p * 4 + j is the slot of block j of prefix p; every slot once.
All inputs are finite; a program needn't handle non-finite values.
Results may differ from a plain program's by a relative error of at most 0.011.
Values may be sent and summed in bfloat16 or wider, within the bound.
A program may use at most 128 MiB of HBM per device.

v0:
```python
import math
import jax
import jax.numpy as jnp
from jax import lax
from jax.sharding import PartitionSpec as P

VH = 32
KH = 16
DK = 128
DV = 128
HQ = 16
KVH = 2
HD = 256
ROT = 64
ROPE_THETA = 10000000.0
YARN_FACTOR = 4.0
YARN_ANCHOR = 262144.0
NEG_LARGE = -1e30
HIGH = lax.Precision.HIGHEST


def carried_in(x, axis, join, neutral):
    place = lax.axis_index(axis)
    gathered = jax.tree.map(
        lambda a, kind: lax.all_gather(a.astype(kind), axis),
        x,
        (jnp.bfloat16, jnp.bfloat16, jnp.bfloat16),
    )
    state = jax.tree.map(lambda a, e: jnp.zeros_like(a) + jnp.asarray(e, a.dtype), x, neutral)

    def one(turn, state):
        return join(
            state,
            jax.tree.map(
                lambda a, own: lax.dynamic_index_in_dim(a, turn, 0, False).astype(own.dtype),
                gathered,
                x,
            ),
        )

    return lax.fori_loop(0, place, one, state)


def yarn_tables(positions, rotary):
    half = rotary // 2
    log_theta = math.log(ROPE_THETA)
    lower = max(
        math.floor(rotary * math.log(YARN_ANCHOR / (64.0 * math.pi)) / (2.0 * log_theta)), 0
    )
    upper = min(
        math.ceil(rotary * math.log(YARN_ANCHOR / (2.0 * math.pi)) / (2.0 * log_theta)), rotary - 1
    )
    spread = float(upper - lower)
    index = jnp.arange(half, dtype=jnp.float32)
    plain_frequency = jnp.exp(index * (-2.0 * log_theta / rotary))
    keep = 1.0 - jnp.clip((index - lower) / spread, 0.0, 1.0)
    frequency = plain_frequency * keep + plain_frequency / YARN_FACTOR * (1.0 - keep)
    angles = positions.astype(jnp.float32)[:, None] * frequency[None, :]
    attention_factor = 0.1 * math.log(YARN_FACTOR) + 1.0
    return (jnp.cos(angles) * attention_factor, jnp.sin(angles) * attention_factor)


def rotate(values, cosines, sines, rotary):
    half = rotary // 2
    first = values[..., :half]
    second = values[..., half:rotary]
    cosines = cosines[:, None, :]
    sines = sines[:, None, :]
    return jnp.concatenate(
        [first * cosines - second * sines, second * cosines + first * sines, values[..., rotary:]],
        axis=-1,
    )


def unit_rows(values):
    return values * lax.rsqrt(jnp.sum(values * values, axis=-1, keepdims=True) + 1e-06)


def row_layout(rows, req_len, req_prefix, req_offset):
    starts = jnp.cumsum(req_len) - req_len
    leading_found = (starts[None, :] <= rows[:, None]).astype(jnp.int32)
    segment = jnp.sum(leading_found, axis=1) - 1
    choose = (segment[:, None] == jnp.arange(req_len.shape[0], dtype=jnp.int32)[None, :]).astype(
        jnp.int32
    )
    first = jnp.sum(choose * starts[None, :], axis=1)
    prefix = jnp.sum(choose * req_prefix[None, :], axis=1)
    offset = jnp.sum(choose * req_offset[None, :], axis=1)
    return (segment, first, prefix, offset, offset + rows - first)


def absorb(state, queries, search_handles, values, visible):
    peak, total, summed = state
    scores = jnp.einsum(
        "thd,nd->thn", queries, search_handles, preferred_element_type=jnp.float32
    ) * search_handles.shape[-1] ** (-0.5)
    seen = visible[:, None, :]
    scores = jnp.where(seen, scores, NEG_LARGE)
    new_peak = jnp.maximum(peak, jnp.max(scores, axis=-1))
    weights = jnp.where(seen, jnp.exp(scores - new_peak[..., None]), 0.0)
    shrink = jnp.exp(peak - new_peak)
    total = total * shrink + jnp.sum(weights, axis=-1)
    summed = summed * shrink[..., None] + jnp.einsum(
        "thn,nd->thd", weights.astype(jnp.bfloat16), values, preferred_element_type=jnp.float32
    )
    return (new_peak, total, summed)


def compose(earlier, later):
    map_early, add_early, flag_early = earlier
    map_late, add_late, flag_late = later
    fresh = flag_late > 0.5
    joined_map = jnp.where(
        fresh, map_late, jnp.einsum("hij,hjk->hik", map_early, map_late, precision=HIGH)
    )
    joined_add = jnp.where(
        fresh, add_late, jnp.einsum("hvj,hjk->hvk", add_early, map_late, precision=HIGH) + add_late
    )
    return (joined_map, joined_add, jnp.maximum(flag_early, flag_late))


def shards(
    dn_query,
    dn_key,
    dn_value,
    dn_gate,
    dn_beta_logit,
    dn_decay,
    dn_norm_gain,
    prefix_state,
    at_query,
    at_gate,
    at_key,
    at_value,
    prefix_key,
    prefix_value,
    req_len,
    req_prefix,
    req_offset,
    block_table,
):
    tokens_here = dn_query.shape[0]
    key_heads = dn_query.shape[1] // DK
    value_heads = dn_value.shape[1] // DV
    query_heads = at_query.shape[1] // HD
    device = lax.axis_index("context")
    row_start = device * tokens_here
    rows = row_start + jnp.arange(tokens_here, dtype=jnp.int32)
    segment, first, prefix, offset, position = row_layout(rows, req_len, req_prefix, req_offset)
    query = jnp.repeat(
        unit_rows(dn_query.reshape(tokens_here, key_heads, DK).astype(jnp.float32)) * DK ** (-0.5),
        VH // KH,
        axis=1,
    )
    key = jnp.repeat(
        unit_rows(dn_key.reshape(tokens_here, key_heads, DK).astype(jnp.float32)), VH // KH, axis=1
    )
    query_heads_first = jnp.transpose(query, (1, 0, 2))
    key_heads_first = jnp.transpose(key, (1, 0, 2))
    value_heads_first = jnp.transpose(
        dn_value.reshape(tokens_here, value_heads, DV).astype(jnp.float32), (1, 0, 2)
    )
    beta = jax.nn.sigmoid(dn_beta_logit).T
    same = segment[:, None] == segment[None, :]
    causal = same & (rows[:, None] >= rows[None, :])
    strict = same & (rows[:, None] > rows[None, :])
    running = jnp.dot(causal.astype(jnp.float32), dn_decay, precision=HIGH).T
    gaps = running[:, :, None] - running[:, None, :]
    decay_mat = jnp.where(causal[None], jnp.exp(jnp.where(causal[None], gaps, 0.0)), 0.0)
    key_gram = jnp.einsum("hid,hjd->hij", key_heads_first, key_heads_first, precision=HIGH)
    query_key = jnp.einsum("hid,hjd->hij", query_heads_first, key_heads_first, precision=HIGH)
    lower_mat = jnp.where(strict[None], beta[:, :, None] * key_gram * decay_mat, 0.0)
    system = jnp.eye(tokens_here, dtype=jnp.float32)[None] + lower_mat
    start_decay = jnp.exp(running)
    solve_values = beta[:, :, None] * value_heads_first
    solve_keys = (beta * start_decay)[:, :, None] * key_heads_first
    solved = jax.scipy.linalg.solve_triangular(
        system, jnp.concatenate([solve_values, solve_keys], axis=2), lower=True, unit_diagonal=True
    )
    update = solved[:, :, :DV]
    wy_keys = solved[:, :, DV:]
    mixing = decay_mat * query_key
    local_out = jnp.einsum("hij,hjv->hiv", mixing, update, precision=HIGH)
    reach = start_decay[:, :, None] * query_heads_first - jnp.einsum(
        "hij,hjk->hik", mixing, wy_keys, precision=HIGH
    )
    tail = segment == segment[tokens_here - 1]
    end_gaps = running[:, tokens_here - 1 : tokens_here] - running
    end_weight = jnp.where(tail[None, :], jnp.exp(jnp.where(tail[None, :], end_gaps, 0.0)), 0.0)
    end_decay = start_decay[:, tokens_here - 1]
    identity_mat = jnp.eye(DK, dtype=jnp.float32)
    carry_map = end_decay[:, None, None] * identity_mat[None] - jnp.einsum(
        "hjk,hj,hjl->hkl", wy_keys, end_weight, key_heads_first, precision=HIGH
    )
    carry_add = jnp.einsum("hjv,hj,hjl->hvl", update, end_weight, key_heads_first, precision=HIGH)
    restart = (first[tokens_here - 1] >= row_start).astype(jnp.float32)
    identity = (
        jnp.broadcast_to(identity_mat, (value_heads, DK, DK)),
        jnp.zeros((value_heads, DV, DK), jnp.float32),
        jnp.zeros((), jnp.float32),
    )
    into_map, into_add, into_flag = carried_in(
        (carry_map, carry_add, restart), "context", compose, identity
    )
    carried = ((segment == segment[0]) & (first[0] < row_start))[None, :, None]
    through = jnp.einsum("hkl,hil->hik", into_map, reach, precision=HIGH)
    extra = jnp.einsum("hvk,hik->hiv", into_add, reach, precision=HIGH)
    weight_vec = jnp.where(carried, through, reach).astype(jnp.bfloat16)
    core = local_out + jnp.where(carried, extra, 0.0)
    owner_ids = jnp.arange(prefix_state.shape[0], dtype=jnp.int32)
    select = (prefix[None, :] == owner_ids[:, None]).astype(jnp.bfloat16)
    masked = select[:, None, :, None] * weight_vec[None]
    state_part = jnp.einsum(
        "phik,phvk->hiv",
        masked,
        lax.all_gather(prefix_state, "context", axis=2, tiled=True),
        preferred_element_type=jnp.float32,
    )
    core = core + state_part
    core_rows = jnp.transpose(core, (1, 0, 2))
    normed = core_rows * lax.rsqrt(jnp.mean(core_rows * core_rows, axis=-1, keepdims=True) + 1e-06)
    gate_rows = dn_gate.reshape(tokens_here, value_heads, DV).astype(jnp.float32)
    dn_out = (
        (normed * dn_norm_gain * jax.nn.silu(gate_rows))
        .reshape(tokens_here, value_heads * DV)
        .astype(jnp.bfloat16)
    )
    group = HQ // KVH
    kv_head = lax.axis_index("head") * query_heads // group
    cosines, sines = yarn_tables(position, ROT)
    query_rot = rotate(
        at_query.reshape(tokens_here, query_heads, HD).astype(jnp.float32), cosines, sines, ROT
    ).astype(jnp.bfloat16)
    new_key = lax.dynamic_slice_in_dim(at_key, kv_head * HD, HD, 1).reshape(tokens_here, 1, HD)
    new_key = (
        rotate(new_key.astype(jnp.float32), cosines, sines, ROT)
        .reshape(tokens_here, HD)
        .astype(jnp.bfloat16)
    )
    new_value = lax.dynamic_slice_in_dim(at_value, kv_head * HD, HD, 1)
    cached_key = lax.dynamic_slice_in_dim(prefix_key, kv_head * HD, HD, 2)
    cached_value = lax.dynamic_slice_in_dim(prefix_value, kv_head * HD, HD, 2)
    table_index = jnp.arange(block_table.shape[0], dtype=jnp.int32)
    blocks_per_prefix = block_table.shape[0] // prefix_state.shape[0]
    state = (
        jnp.full((tokens_here, query_heads), NEG_LARGE, jnp.float32),
        jnp.zeros((tokens_here, query_heads), jnp.float32),
        jnp.zeros((tokens_here, query_heads, HD), jnp.float32),
    )
    search_handles = lax.all_gather(cached_key, "context", axis=0, tiled=True)
    values = lax.all_gather(cached_value, "context", axis=0, tiled=True)
    count = search_handles.shape[0]
    width = search_handles.shape[1]
    slots = jnp.arange(count, dtype=jnp.int32)
    entry = jnp.sum(
        jnp.where(block_table[None, :] == slots[:, None], table_index[None, :], 0), axis=1
    )
    owner = jnp.repeat(entry // blocks_per_prefix, width)
    where_in = (
        (entry % blocks_per_prefix)[:, None] * width + jnp.arange(width, dtype=jnp.int32)[None, :]
    ).reshape(count * width)
    visible = (owner[None, :] == prefix[:, None]) & (where_in[None, :] < offset[:, None])
    flat_keys = search_handles.reshape(count * width, search_handles.shape[2])
    flat_values = values.reshape(count * width, values.shape[2])
    state = absorb(state, query_rot, flat_keys, flat_values, visible)
    search_handles = lax.all_gather(new_key, "context", axis=0, tiled=True)
    values = lax.all_gather(new_value, "context", axis=0, tiled=True)
    key_rows = jnp.arange(search_handles.shape[0], dtype=jnp.int32)
    key_segment = row_layout(key_rows, req_len, req_prefix, req_offset)[0]
    visible = (key_segment[None, :] == segment[:, None]) & (key_rows[None, :] <= rows[:, None])
    state = absorb(state, query_rot, search_handles, values, visible)
    peak, total, summed = state
    attention = summed / total[..., None]
    gate_att = at_gate.reshape(tokens_here, query_heads, HD).astype(jnp.float32)
    at_out = (
        (attention * jax.nn.sigmoid(gate_att))
        .reshape(tokens_here, query_heads * HD)
        .astype(jnp.bfloat16)
    )
    return (dn_out, at_out)


def solution(mesh):
    placed = (
        P(("group", "context"), "head"),
        P(("group", "context"), "head"),
        P(("group", "context"), "head"),
        P(("group", "context"), "head"),
        P(("group", "context"), "head"),
        P(("group", "context"), "head"),
        P(),
        P("group", "head", "context", None),
        P(("group", "context"), "head"),
        P(("group", "context"), "head"),
        P(("group", "context"), None),
        P(("group", "context"), None),
        P(("group", "context"), None, None),
        P(("group", "context"), None, None),
        P("group"),
        P("group"),
        P("group"),
        P("group"),
    )
    return jax.shard_map(
        shards,
        mesh=mesh,
        in_specs=placed,
        out_specs=(P(("group", "context"), "head"), P(("group", "context"), "head")),
        check_vma=False,
    )
```

profile of v0, /device:TPU:26, one launch (start us, length us, event | category | flops | bytes accessed | tf_op | source)
XLA Modules:
  0.0 243.3 jit_solution(15976261732324481945)
XLA Ops:
  12.8 2.1 fusion.15
  14.9 79.4 %custom-call.4 = f32[8,1,128,128]{2,3,1,0:T(8,128)S(1)} custom-call(f32[8,1,128,128]{3,2,1,0:T(8,128)} %fusion.15), custom_call_target="InvertDiagBlocksLowerTriangular" | custom-call | tf_op jit(solution)/shard_map/jit(_solve_triangular)/vmap()/triangular_solve | solution.py:177
  94.3 1.8 compare_and_fusion.3
  96.7 1.0 fusion.22
  97.8 1.7 convolution_convert_fusion
  99.8 1.7 fusion.20
  104.2 16.7 %all-gather.2 = bf16[512,1,256]{0,2,1:T(8,128)(2,1)} all-gather(bf16[128,1,256]{0,2,1:T(8,128)(2,1)S(1)} %pad_maximum_fusion.1), channel_id=4, replica_groups=mesh['group'=2,'context'=4,'head'=4] {'context'}, dimensions={0}, use_global_device_ids=true | all-gather | bytes 327680 | tf_op jit(solution)/shard_map/all_gather | solution.py:266
  121.9 16.6 %all_gather.40 = bf16[8,64,256]{2,1,0:T(8,128)(2,1)} all-gather(bf16[2,64,256]{2,1,0:T(8,128)(2,1)S(1)} %constant_dynamic-slice_fusion.3), channel_id=1, replica_groups=mesh['group'=2,'context'=4,'head'=4] {'context'}, dimensions={0}, use_global_device_ids=true | all-gather | bytes 327680 | tf_op jit(solution)/shard_map/all_gather | solution.py:250
  138.9 16.8 %all_gather.41 = bf16[8,64,256]{2,1,0:T(8,128)(2,1)} all-gather(bf16[2,64,256]{2,1,0:T(8,128)(2,1)S(1)} %constant_dynamic-slice_fusion.2), channel_id=1, replica_groups=mesh['group'=2,'context'=4,'head'=4] {'context'}, dimensions={0}, use_global_device_ids=true | all-gather | bytes 327680 | tf_op jit(solution)/shard_map/all_gather | solution.py:251
  155.7 16.5 %all_gather.43 = bf16[512,256]{1,0:T(8,128)(2,1)} all-gather(bf16[128,256]{1,0:T(8,128)(2,1)S(1)} %constant_dynamic-slice_fusion.4), channel_id=1, replica_groups=mesh['group'=2,'context'=4,'head'=4] {'context'}, dimensions={0}, use_global_device_ids=true | all-gather | bytes 327680 | tf_op jit(solution)/shard_map/all_gather | solution.py:267
  172.5 1.0 copy.164
  180.1 1.2 fusion.18
  181.8 1.9 dynamic-update-slice
  183.7 2.3 fusion.19
  186.6 8.6 %all-reduce = bf16[4]{0:T(256)(128)(2,1)} all-reduce(bf16[4]{0:T(256)(128)(2,1)S(1)} %copy-done.39), channel_id=1, replica_groups=mesh['group'=2,'context'=4,'head'=4] {'context'}, use_global_device_ids=true, to_apply=%add | all-reduce | flops 4 | bytes 16
  195.3 1.1 copy.165
  198.4 0.9 copy-done.13
  199.7 15.1 %all_gather.39 = bf16[2,8,128,128]{3,2,0,1:T(8,128)(2,1)S(1)} all-gather(bf16[2,8,32,128]{3,2,0,1:T(8,128)(2,1)S(1)} %copy.150), channel_id=1, replica_groups=mesh['group'=2,'context'=4,'head'=4] {'context'}, dimensions={2}, use_global_device_ids=true | all-gather | bytes 655360 | tf_op jit(solution)/shard_map/all_gather | solution.py:216
  216.1 1.2 convolution_multiply_fusion.3
  217.3 1.5 fusion.43
  220.2 11.2 %while.14 = (s32[]{:T(128)}, f32[8,128,128]{1,2,0:T(8,128)S(1)}, f32[8,128,128]{1,2,0:T(8,128)S(1)}, s32[]{:T(128)}, bf16[4]{0:T(256)(128)(2,1)S(1)}, /*index=5*...) while((s32[]{:T(128)}, f32[8,128,128]{1,2,0:T(8,128)S(1)}, ...), condition=%wide.region_6.7_spmd, body=%wide.region_5.6_spmd.sunk | while | flops 403308544 | bytes 7340196 | solution.py:41
  220.2 1.1 constant_dynamic-slice_fusion.7
  223.9 1.1 constant_dynamic-slice_fusion.7
  227.7 1.1 constant_dynamic-slice_fusion.7
  (191 shorter events, 32.6 us)
Async XLA Ops:
  7.2 96.5 %copy-start = (bf16[128,512]{1,0:T(8,128)(2,1)S(1)}, bf16[128,512]{1,0:T(8,128)(2,1)}, u32[]{:S(2)}) copy-start(bf16[128,512]{1,0:T(8,128)(2,1)} %param.30) | copy-start | bytes 393220
  7.2 212.3 %all-gather.8.cloned.1.call-start = ((), (), s32[]{:S(2)}) async-start(), calls=%async_computation.1 | async-start | bytes 1310720 | tf_op jit(solution)/shard_map/all_gather | solution.py:25
  7.2 3.6 %copy-start.15 = (bf16[128,512]{1,0:T(8,128)(2,1)S(1)}, bf16[128,512]{1,0:T(8,128)(2,1)}, u32[]{:S(2)}) copy-start(bf16[128,512]{1,0:T(8,128)(2,1)} %param.21) | copy-start | bytes 393220
  7.3 92.5 %copy-start.2 = (f32[128,128]{1,0:T(8,128)}, f32[128,128]{1,0:T(8,128)S(1)}, u32[]{:S(2)}) copy-start(f32[128,128]{1,0:T(8,128)S(1)} %get-tuple-element.158) | copy-start | bytes 196612
  9.0 166.3 %copy-start.28 = (s32[128]{0:T(128)}, s32[128]{0:T(128)S(1)}, u32[]{:S(2)}) copy-start(s32[128]{0:T(128)S(1)} %get-tuple-element.108) | copy-start | bytes 1540
  9.0 1.3 copy-start.34
  10.6 85.6 %copy-start.18 = (f32[8,128]{1,0:T(8,128)}, f32[8,128]{1,0:T(8,128)S(1)}, u32[]{:S(2)}) copy-start(f32[8,128]{1,0:T(8,128)S(1)} %convolution_bitcast_fusion.3) | copy-start | bytes 12292
  11.4 1.0 copy-start.10
  96.2 3.4 %copy-start.20 = (f32[8,128]{1,0:T(8,128)}, f32[8,128]{1,0:T(8,128)S(1)}, u32[]{:S(2)}) copy-start(f32[8,128]{1,0:T(8,128)S(1)} %get-tuple-element.135) | copy-start | bytes 12292
  99.5 120.0 %all-gather.6.cloned.1.call-start = ((), (), s32[]{:S(2)}) async-start(), calls=%async_computation | async-start | bytes 1310720 | tf_op jit(solution)/shard_map/all_gather | solution.py:25
  120.9 1.0 copy-start.22
  121.9 16.6 %copy-start.36 = (s32[8]{0:T(128)S(1)}, s32[8]{0:T(128)}, u32[]{:S(2)}) copy-start(s32[8]{0:T(128)} %param.37) | copy-start | bytes 100
  121.9 17.0 %copy-start.23 = (bf16[2,64,512]{2,1,0:T(8,128)(2,1)S(1)}, bf16[2,64,512]{2,1,0:T(8,128)(2,1)}, u32[]{:S(2)}) copy-start(bf16[2,64,512]{2,1,0:T(8,128)(2,1)} %param.33) | copy-start | bytes 393220
  138.9 16.8 %copy-start.24 = (bf16[128,512]{1,0:T(8,128)(2,1)S(1)}, bf16[128,512]{1,0:T(8,128)(2,1)}, u32[]{:S(2)}) copy-start(bf16[128,512]{1,0:T(8,128)(2,1)} %param.31) | copy-start | bytes 393220
  155.7 16.5 %copy-start.12 = (bf16[128,1024]{1,0:T(8,128)(2,1)S(1)}, bf16[128,1024]{1,0:T(8,128)(2,1)}, u32[]{:S(2)}) copy-start(bf16[128,1024]{1,0:T(8,128)(2,1)} %param.29) | copy-start | bytes 786436
  172.5 1.0 copy-start.16
  175.2 1.0 copy-start.14
  178.2 1.9 copy-start.6
  180.1 3.6 %copy-start.4 = (f32[128,4,256]{2,0,1:T(8,128)S(1)}, f32[128,4,256]{2,0,1:T(8,128)}, u32[]{:S(2)}) copy-start(f32[128,4,256]{2,0,1:T(8,128)} %copy.164) | copy-start | bytes 1572868
  183.7 2.3 copy-start.9
  186.0 9.2 %copy-start.3 = (f32[128,128]{1,0:T(8,128)S(1)}, f32[128,128]{1,0:T(8,128)}, u32[]{:S(2)}) copy-start(f32[128,128]{1,0:T(8,128)} %copy-done.2) | copy-start | bytes 196612
  199.7 15.2 %copy-start.29 = (s32[128]{0:T(128)S(1)}, s32[128]{0:T(128)}, u32[]{:S(2)}) copy-start(s32[128]{0:T(128)} %copy-done.28) | copy-start | bytes 1540
  217.3 1.5 copy-start.21
  232.7 1.0 copy-start.1
  (18 other events, 13.3 us)
Sparse Core Ops, SparseCore 0:
  99.7 32.8 all-gather.7
  134.7 33.2 all-gather.5
where the time goes:
time: 244 us; the launch traced here: 243 us
  blocking collectives  90.3 us (37%)
  other arithmetic  87.6 us (36%)
  local copies, waits for them, and re-layouts  27.8 us (11%)
  matrix products  19.2 us (8%)
  between operations  16.1 us (7%)
    another operation x2, other arithmetic, shards(): jax.scipy.linalg.solve_triangular(system, jnp.concatenate([solve_values,...  79.4 us
    all_gather x1, blocking collectives, shards(): values = lax.all_gather(cached_value, 'context', axis=0, tiled=True)  16.8 us
    all_gather x1, blocking collectives, shards(): search_handles = lax.all_gather(new_key, 'context', axis=0, tiled=True)  16.7 us
    all_gather x1, blocking collectives, shards(): search_handles = lax.all_gather(cached_key, 'context', axis=0, tiled=True)  16.6 us
    all_gather x1, blocking collectives, shards(): values = lax.all_gather(new_value, 'context', axis=0, tiled=True)  16.5 us
    unnamed x91, local copies, waits for them, and re-layouts  15.3 us
    all_gather x1, blocking collectives, shards(): lax.all_gather(prefix_state, 'context', axis=2, tiled=True)  15.1 us
    unnamed x1, blocking collectives  8.58 us
  transfers between devices with their start and end apart: 2, of which 0 were waited for; matrix products, arithmetic and copies ran while one was open for 9% of the time, Pallas kernels for 0%

commit v1 on v0

--- a/solution.py
+++ b/solution.py
@@ -17,6 +17,19 @@
 YARN_ANCHOR = 262144.0
 NEG_LARGE = -1e30
 HIGH = lax.Precision.HIGHEST
+
+
+def gather_around(array, axis, dim):
+    ways = lax.axis_size(axis)
+    up = [(d, (d + 1) % ways) for d in range(ways)]
+    down = [(d, (d - 1) % ways) for d in range(ways)]
+    earlier, later = ([array], [array])
+    for _ in range(ways // 2):
+        earlier.append(lax.ppermute(earlier[-1], axis, up))
+    for _ in range((ways - 1) // 2):
+        later.append(lax.ppermute(later[-1], axis, down))
+    line = jnp.concatenate([*earlier[::-1], *later[1:]], axis=dim)
+    return jnp.roll(line, (lax.axis_index(axis) - ways // 2) * array.shape[dim], axis=dim)
 
 
 def carried_in(x, axis, join, neutral):
@@ -264,7 +277,7 @@
     flat_values = values.reshape(count * width, values.shape[2])
     state = absorb(state, query_rot, flat_keys, flat_values, visible)
     search_handles = lax.all_gather(new_key, "context", axis=0, tiled=True)
-    values = lax.all_gather(new_value, "context", axis=0, tiled=True)
+    values = gather_around(new_value, "context", 0)
     key_rows = jnp.arange(search_handles.shape[0], dtype=jnp.int32)
     key_segment = row_layout(key_rows, req_len, req_prefix, req_offset)[0]
     visible = (key_segment[None, :] == segment[:, None]) & (key_rows[None, :] <= rows[:, None])

time: 244 us -> 227 us (0.930)
  blocking collectives: 90.3 us -> 72.5 us
  starting transfers between devices: 0.08 us -> 3.99 us
  other arithmetic: 87.6 us -> 83.9 us
  local copies, waits for them, and re-layouts: 27.8 us -> 30.6 us
    all_gather x1 -> x0, blocking collectives: 16.5 us -> none  [shards(): values = lax.all_gather(new_value, 'context', axis=0, tiled=True)]
    ppermute x0 -> x3, starting transfers between devices: none -> 3.91 us  [the longest x2 2.11 us: gather_around(): earlier.append(lax.ppermute(earlier[-1], axis, up))]
    unnamed x91 -> x74, local copies, waits for them, and re-layouts: 15.3 us -> 17.5 us
  transfers between devices with their start and end apart: 2 -> 5, of which waited for: 0 -> 0; matrix products, arithmetic and copies ran while one was open for 9% -> 11% of each run, Pallas kernels for 0% -> 0%
where the time goes in v1:
time: 227 us; the launch traced here: 226 us
  other arithmetic  83.9 us (37%)
  blocking collectives  72.5 us (32%)
  local copies, waits for them, and re-layouts  30.6 us (13%)
  matrix products  17.2 us (8%)
  between operations  16 us (7%)
  starting transfers between devices  3.99 us (2%)
    another operation x2, other arithmetic, shards(): jax.scipy.linalg.solve_triangular(system, jnp.concatenate([solve_values,...  78.6 us
    unnamed x74, local copies, waits for them, and re-layouts  17.5 us
    all_gather x1, blocking collectives, shards(): values = lax.all_gather(cached_value, 'context', axis=0, tiled=True)  16.7 us
    all_gather x1, blocking collectives, shards(): search_handles = lax.all_gather(new_key, 'context', axis=0, tiled=True)  16.7 us
    all_gather x1, blocking collectives, shards(): search_handles = lax.all_gather(cached_key, 'context', axis=0, tiled=True)  15.6 us
    all_gather x1, blocking collectives, shards(): lax.all_gather(prefix_state, 'context', axis=2, tiled=True)  14.8 us
    unnamed x1, blocking collectives  8.62 us
    dynamic_slice x12, local copies, waits for them, and re-layouts, one(): lax.dynamic_index_in_dim(a, turn, 0, False).astype(own.dtype)  6.04 us
  transfers between devices with their start and end apart: 5, of which 0 were waited for; matrix products, arithmetic and copies ran while one was open for 11% of the time, Pallas kernels for 0%

profile of v1, /device:TPU:26, one launch (start us, length us, event | category | flops | bytes accessed | tf_op | source)
XLA Modules:
  0.0 226.3 jit_solution(2586210909350464604)
XLA Ops:
  12.7 1.3 fusion.15
  14.0 78.6 %custom-call.4 = f32[8,1,128,128]{2,3,1,0:T(8,128)S(1)} custom-call(f32[8,1,128,128]{3,2,1,0:T(8,128)S(1)} %fusion.15), custom_call_target="InvertDiagBlocksLowerTriangular" | custom-call | tf_op jit(solution)/shard_map/jit(_solve_triangular)/vmap()/triangular_solve | solution.py:190
  92.6 1.3 compare_and_fusion.3
  94.5 1.0 fusion.22
  95.5 1.7 convolution_convert_fusion
  99.0 1.8 collective-permute-start.2
  101.0 1.7 fusion.20
  105.6 1.2 convolution_multiply_fusion.3
  106.8 1.5 fusion.43
  109.4 16.7 %all-gather.2 = bf16[512,1,256]{0,2,1:T(8,128)(2,1)S(1)} all-gather(bf16[128,1,256]{0,2,1:T(8,128)(2,1)S(1)} %pad_maximum_fusion.1), channel_id=4, replica_groups=mesh['group'=2,'context'=4,'head'=4] {'context'}, dimensions={0}, use_global_device_ids=true | all-gather | bytes 327680 | tf_op jit(solution)/shard_map/all_gather | solution.py:279
  127.0 15.6 %all_gather.37 = bf16[8,64,256]{2,1,0:T(8,128)(2,1)} all-gather(bf16[2,64,256]{2,1,0:T(8,128)(2,1)S(1)} %constant_dynamic-slice_fusion.5), channel_id=1, replica_groups=mesh['group'=2,'context'=4,'head'=4] {'context'}, dimensions={0}, use_global_device_ids=true | all-gather | bytes 327680 | tf_op jit(solution)/shard_map/all_gather | solution.py:263
  143.1 16.7 %all_gather.38 = bf16[8,64,256]{2,1,0:T(8,128)(2,1)} all-gather(bf16[2,64,256]{2,1,0:T(8,128)(2,1)S(1)} %constant_dynamic-slice_fusion.4), channel_id=1, replica_groups=mesh['group'=2,'context'=4,'head'=4] {'context'}, dimensions={0}, use_global_device_ids=true | all-gather | bytes 327680 | tf_op jit(solution)/shard_map/all_gather | solution.py:264
  163.5 1.2 fusion.18
  167.2 1.9 collective-permute-start.1
  169.1 14.8 %all_gather.36 = bf16[2,8,128,128]{3,2,0,1:T(8,128)(2,1)S(1)} all-gather(bf16[2,8,32,128]{3,2,0,1:T(8,128)(2,1)S(1)} %copy.150), channel_id=1, replica_groups=mesh['group'=2,'context'=4,'head'=4] {'context'}, dimensions={2}, use_global_device_ids=true | all-gather | bytes 655360 | tf_op jit(solution)/shard_map/all_gather | solution.py:229
  183.9 8.6 %all-reduce = bf16[4]{0:T(256)(128)(2,1)} all-reduce(bf16[4]{0:T(256)(128)(2,1)S(1)} %dynamic-update-slice), channel_id=1, replica_groups=mesh['group'=2,'context'=4,'head'=4] {'context'}, use_global_device_ids=true, to_apply=%add | all-reduce | flops 4 | bytes 16
  193.5 1.1 copy.152
  194.8 0.9 constant_dynamic-update-slice_fusion.7
  200.0 1.1 fusion.19
  201.1 1.1 copy.165
  203.8 11.3 %while.14 = (s32[]{:T(128)}, f32[8,128,128]{1,2,0:T(8,128)S(1)}, f32[8,128,128]{1,2,0:T(8,128)S(1)}, s32[]{:T(128)}, bf16[4]{0:T(256)(128)(2,1)S(1)}, /*index=5*...) while((s32[]{:T(128)}, f32[8,128,128]{1,2,0:T(8,128)S(1)}, ...), condition=%wide.region_6.7_spmd, body=%wide.region_5.6_spmd.sunk | while | flops 403308544 | bytes 7340196 | solution.py:54
  203.8 1.1 constant_dynamic-slice_fusion.7
  207.5 1.1 constant_dynamic-slice_fusion.7
  211.3 1.1 constant_dynamic-slice_fusion.7
  (180 shorter events, 35.1 us)
Async XLA Ops:
  7.2 101.8 %copy-start = (bf16[128,512]{1,0:T(8,128)(2,1)S(1)}, bf16[128,512]{1,0:T(8,128)(2,1)}, u32[]{:S(2)}) copy-start(bf16[128,512]{1,0:T(8,128)(2,1)} %param.30) | copy-start | bytes 393220
  7.2 195.9 %all-gather.8.cloned.1.call-start = ((), (), s32[]{:S(2)}) async-start(), calls=%async_computation.1 | async-start | bytes 1310720 | tf_op jit(solution)/shard_map/all_gather | solution.py:38
  7.2 3.5 %copy-start.13 = (bf16[128,512]{1,0:T(8,128)(2,1)S(1)}, bf16[128,512]{1,0:T(8,128)(2,1)}, u32[]{:S(2)}) copy-start(bf16[128,512]{1,0:T(8,128)(2,1)} %param.21) | copy-start | bytes 393220
  9.0 1.3 copy-start.22
  11.3 1.0 copy-start.9
  97.3 0.9 copy-start.2
  97.3 105.8 %all-gather.6.cloned.1.call-start = ((), (), s32[]{:S(2)}) async-start(), calls=%async_computation | async-start | bytes 1310720 | tf_op jit(solution)/shard_map/all_gather | solution.py:38
  98.8 68.4 %collective-permute-start = (bf16[128,256]{1,0:T(8,128)(2,1)}, bf16[128,256]{1,0:T(8,128)(2,1)}, u32[]{:S(2)}, u32[]{:S(2)}) collective-permute-start(bf16[128,256]{1,0:T(8,128)(2,1)} %constant_dynamic-slice_fusion.2), channel_id=1, source_target_pairs={{0,4},{4,8},{8,12},{12,0},{1,5},{5,9},{9,13},{13,1},{2,6},{6,10},{... | collective-permute-start | bytes 196616 | tf_op jit(solution)/shard_map/ppermute | solution.py:28
  99.0 97.6 %collective-permute-start.2 = (bf16[128,256]{1,0:T(8,128)(2,1)}, bf16[128,256]{1,0:T(8,128)(2,1)}, u32[]{:S(2)}, u32[]{:S(2)}) collective-permute-start(bf16[128,256]{1,0:T(8,128)(2,1)} %constant_dynamic-slice_fusion.2), channel_id=1, source_target_pairs={{0,12},{4,0},{8,4},{12,8},{1,13},{5,1},{9,5},{13,9},{2,14},{6,2},{... | collective-permute-start | bytes 196616 | tf_op jit(solution)/shard_map/ppermute | solution.py:30
  102.7 0.9 copy-start.10
  104.1 0.9 copy-start.14
  126.1 0.9 copy-start.16
  127.0 35.5 %copy-start.6 = (pred[128,512]{1,0:T(8,128)(4,1)}, pred[128,512]{1,0:T(8,128)(4,1)S(1)}, u32[]{:S(2)}) copy-start(pred[128,512]{1,0:T(8,128)(4,1)S(1)} %fusion.50) | copy-start | bytes 196612
  127.0 15.6 %copy-start.24 = (s32[8]{0:T(128)S(1)}, s32[8]{0:T(128)}, u32[]{:S(2)}) copy-start(s32[8]{0:T(128)} %param.37) | copy-start | bytes 100
  127.0 16.1 %copy-start.17 = (bf16[2,64,512]{2,1,0:T(8,128)(2,1)S(1)}, bf16[2,64,512]{2,1,0:T(8,128)(2,1)}, u32[]{:S(2)}) copy-start(bf16[2,64,512]{2,1,0:T(8,128)(2,1)} %param.33) | copy-start | bytes 393220
  142.7 17.1 %copy-start.11 = (bf16[128,1024]{1,0:T(8,128)(2,1)S(1)}, bf16[128,1024]{1,0:T(8,128)(2,1)}, u32[]{:S(2)}) copy-start(bf16[128,1024]{1,0:T(8,128)(2,1)} %param.29) | copy-start | bytes 786436
  160.1 1.0 copy-start.12
  161.1 0.9 copy-start.5
  162.5 1.0 copy-start.4
  163.5 1.8 copy-start.15
  167.2 27.6 %collective-permute-start.1 = (bf16[128,256]{1,0:T(8,128)(2,1)}, bf16[128,256]{1,0:T(8,128)(2,1)}, u32[]{:S(2)}, u32[]{:S(2)}) collective-permute-start(bf16[128,256]{1,0:T(8,128)(2,1)} %collective-permute-done), channel_id=1, source_target_pairs={{0,4},{4,8},{8,12},{12,0},{1,5},{5,9},{9,13},{13,1},{2,6},{6,10},{... | collective-permute-start | bytes 196616 | tf_op jit(solution)/shard_map/ppermute | solution.py:28
  194.8 1.8 copy-start.3
  194.8 5.2 %copy-start.27 = (f32[128,4,256]{2,0,1:T(8,128)S(1)}, f32[128,4,256]{2,0,1:T(8,128)}, u32[]{:S(2)}) copy-start(f32[128,4,256]{2,0,1:T(8,128)} %fusion.18) | copy-start | bytes 1572868
  215.7 1.0 copy-start.1
  (9 other events, 6.4 us)
Sparse Core Ops, SparseCore 0:
  97.4 31.6 all-gather.7
  131.3 32.1 all-gather.5
